TPU v7x, 32 devices: a whole 2x2x4 slice. The times are simulated.
32 devices in a mesh: grp: 2 (over x), date: 16 (over z, y, core).
Axes of the slice: x: 2, y: 2, z: 4, core: 2. Of those that a mesh axis runs over, the one named last changes fastest.
Arguments:
- radar_stack: bfloat16 [2, 128, 256, 256], P(None, 'date', 'grp'), parts along dimension 2, may hold values from -6 to 6
- filter_taps: float32 [2, 128, 128], P(None, 'date'), may hold values from -0.6 to 0.6
- filter_lengths: int32 [128], P('date'), may hold values from 64 to 128
- resample_kernel: float32 [4], replicated, may hold values from 0.2 to 1
- tile_owner: int32 [512, 1], P(('grp', 'date')), parts along dimension 0, may hold values from 0 to 15; in each aligned block of 16 rows (0 to 15, 16 to 31, ...) at most 2 rows name the same one
- map_slot: int32 [512], P(('grp', 'date')), parts along dimension 0, may hold values from 0 to 7
- correlation: int32 [512], P(('grp', 'date')), parts along dimension 0, may hold values from 1 to 128
- offsets: int32 [512], P(('grp', 'date')), parts along dimension 0, may hold values from 0 to 127
Outputs:
- geocoded: float32 [256, 256, 128], P(('grp', 'date')), parts along dimension 0
There are 2 independent parts, one for each index of `grp`. A program takes and returns all parts, laid end to end along the dimension named above; an argument that names none is the same for every part. Nothing has to cross between parts.
Inputs may be any that keep to these rules, and one draw needn't show every extreme that they name: `tile_owner`: among the 16 tiles of one device, at most 2 name the same owner.
All inputs are finite; a program needn't handle non-finite values. Where the computation divides by a largest or mean magnitude, that divisor is 1e-20 or more.
Results may differ from a plain program's by a relative error of at most 0.0055.
Values may be sent and summed in bfloat16 or wider, within the bound.
A program may use at most 64 MiB of HBM per device.

v0:
```python
from functools import partial

import jax
import jax.numpy as jnp
from jax import lax
from jax.experimental import pallas as pl
from jax.experimental.pallas import tpu as pltpu
from jax.sharding import PartitionSpec as P

PATCH_AZ = 8
PATCH_RG = 16
TILE = 128
KW = 4
CAP = 2
MAP_DEV = 8
LANES = 128

diag_load = 0.5
small_eps = 1e-05
MESH = pl.DeviceIdType.MESH
VMEM = pl.BlockSpec(memory_space=pltpu.VMEM)
SMEM = pl.BlockSpec(memory_space=pltpu.SMEM)
BIG = 60 * 1024 * 1024


def block_transpose(parts, group):
    count = len(parts)
    lane = lax.broadcasted_iota(jnp.int32, parts[0].shape, 1) // group
    bit = 1
    while bit < count:
        low = (lane // bit) % 2 == 0
        new = list(parts)
        for a in range(count):
            if a & bit == 0:
                x, y = parts[a], parts[a | bit]
                new[a] = jnp.where(low, x, pltpu.roll(y, bit * group, 1))
                new[a | bit] = jnp.where(low, pltpu.roll(x, LANES - bit * group, 1), y)
        parts = new
        bit *= 2
    return parts


def filter_kernel(n, len_ref, radar_ref, taps_ref, out_ref, rows_ref):
    dates, rows = radar_ref.shape[1], radar_ref.shape[2]
    taps = taps_ref.shape[2]
    halves = out_ref.shape[1]
    position = lax.broadcasted_iota(jnp.int32, (1, taps), 1)
    a_iota = lax.broadcasted_iota(jnp.int32, (rows, rows), 0)
    b_iota = lax.broadcasted_iota(jnp.int32, (rows, rows), 1)
    at = b_iota - a_iota + taps // 2
    inside = jnp.logical_and(at >= 0, at < taps)
    for d in range(dates):

        def toeplitz(which):
            h = jnp.where(position < len_ref[d], taps_ref[which, pl.ds(d, 1), :], 0.0)
            wide = jnp.broadcast_to(h, (rows, taps))
            rolled = pltpu.roll(wide, taps // 2, 1, stride=1, stride_axis=0)
            full = jnp.concatenate([rolled] * (rows // taps), axis=1)
            return jnp.where(inside, full, 0.0)

        t_re, t_im = toeplitz(0), toeplitz(1)
        operator = jnp.concatenate(
            [jnp.concatenate([t_re, -t_im], axis=1), jnp.concatenate([t_im, t_re], axis=1)], axis=0
        ).astype(jnp.bfloat16)
        columns = jnp.concatenate([radar_ref[0, d], radar_ref[1, d]], axis=0)
        product = jnp.dot(operator, columns, preferred_element_type=jnp.float32)
        for c in range(halves):
            for p in range(n):
                for part in range(2):
                    top = part * rows + p * PATCH_AZ
                    rows_ref[c, p, pl.ds(part * PATCH_AZ * dates + d, PATCH_AZ, stride=dates), :] = (
                        product[top : top + PATCH_AZ, c * LANES : (c + 1) * LANES]
                    )
    for c in range(halves):
        for p in range(n):
            out_ref[p, c] = rows_ref[c, p].astype(jnp.bfloat16)


def exchange_kernel(n, count, *refs):
    ins, outs = refs[:count], refs[count : 2 * count]
    send_sem, recv_sem, own_sem = refs[2 * count :]
    me = lax.axis_index("date")
    barrier = pltpu.get_barrier_semaphore()
    for k in range(1, n):
        peer = lax.rem(me + k, n)
        pl.semaphore_signal(barrier, inc=1, device_id={"date": peer}, device_id_type=MESH)
    own = [
        pltpu.make_async_copy(x.at[me], y.at[me], own_sem.at[i])
        for i, (x, y) in enumerate(zip(ins, outs))
    ]
    for copy in own:
        copy.start()
    pl.semaphore_wait(barrier, n - 1)

    def outgoing(i, peer):
        return pltpu.make_async_remote_copy(
            src_ref=ins[i].at[peer],
            dst_ref=outs[i].at[me],
            send_sem=send_sem.at[i, peer],
            recv_sem=recv_sem.at[i, me],
            device_id={"date": peer},
            device_id_type=MESH,
        )

    def incoming(i, peer):
        return pltpu.make_async_remote_copy(
            src_ref=ins[i].at[peer],
            dst_ref=outs[i].at[peer],
            send_sem=send_sem.at[i, peer],
            recv_sem=recv_sem.at[i, peer],
            device_id={"date": peer},
            device_id_type=MESH,
        )

    for k in range(1, n):
        for i in range(count):
            outgoing(i, lax.rem(me + k, n)).start()
    for k in range(1, n):
        for i in range(count):
            incoming(i, lax.rem(me + n - k, n)).wait_recv()
    for k in range(1, n):
        for i in range(count):
            outgoing(i, lax.rem(me + k, n)).wait_send()
    for copy in own:
        copy.wait()


def exchange(n, collective, *arrays):
    count = len(arrays)
    return pl.pallas_call(
        partial(exchange_kernel, n, count),
        out_shape=[jax.ShapeDtypeStruct(x.shape, x.dtype) for x in arrays],
        in_specs=[VMEM] * count,
        out_specs=[VMEM] * count,
        scratch_shapes=[
            pltpu.SemaphoreType.DMA((count, n)),
            pltpu.SemaphoreType.DMA((count, n)),
            pltpu.SemaphoreType.DMA((count,)),
        ],
        compiler_params=pltpu.CompilerParams(collective_id=collective, has_side_effects=True, vmem_limit_bytes=BIG),
        name="exchange%d" % collective,
    )(*arrays)


def whiten_window(z):
    dates, looks = z.shape[0] // 2, z.shape[1]
    gram = lax.dot_general(z, z, (((1,), (1,)), ((), ())), preferred_element_type=jnp.float32)
    gram_re = (gram[:dates, :dates] + gram[dates:, dates:]) * (1.0 / looks)
    gram_im = (gram[dates:, :dates] - gram[:dates, dates:]) * (1.0 / looks)
    eye = lax.broadcasted_iota(jnp.int32, (dates, dates), 0) == lax.broadcasted_iota(
        jnp.int32, (dates, dates), 1
    )
    diagonal = jnp.where(eye, gram_re, 0.0)
    scale_col = lax.rsqrt(jnp.sum(diagonal, axis=1, keepdims=True) + small_eps)
    scale_row = lax.rsqrt(jnp.sum(diagonal, axis=0, keepdims=True) + small_eps)
    outer = scale_col * scale_row
    coher_re = gram_re * outer + jnp.where(eye, diag_load, 0.0)
    coher_im = gram_im * outer
    sums = jnp.sum(jnp.abs(coher_re) + jnp.abs(coher_im), axis=1, keepdims=True)
    over = 1.0 / jnp.max(sums, axis=0, keepdims=True)

    def embed(re, im):
        re, im = re.astype(jnp.bfloat16), im.astype(jnp.bfloat16)
        top = jnp.concatenate([re, -im], axis=1)
        return top, jnp.concatenate([top, jnp.concatenate([im, re], axis=1)], axis=0)

    part_re, part_im = coher_re * over, coher_im * over
    stages = []
    for stage in range(3):
        top, whole = embed(part_re, part_im)
        stages.append(whole)
        if stage < 2:
            square = jnp.dot(top, whole, preferred_element_type=jnp.float32)
            part_re = 2.0 * part_re - square[:, :dates]
            part_im = 2.0 * part_im + square[:, dates:]
    w = z.astype(jnp.float32)
    for whole in reversed(stages):
        w = 2.0 * w - jnp.dot(whole, w.astype(jnp.bfloat16), preferred_element_type=jnp.float32)
    return w * over


def whiten_kernel(n, table_ref, x_ref, out_ref, z_ref, tiles_ref):
    halves, rows = x_ref.shape[1], x_ref.shape[2]
    dates_here = rows // (2 * PATCH_AZ)
    total = n * dates_here
    per_half = LANES // PATCH_RG
    for s in range(n):
        for c in range(halves):
            x = x_ref[s, c].astype(jnp.float32)
            lines = []
            for a in range(PATCH_AZ):
                re = x[a * dates_here : (a + 1) * dates_here]
                start = PATCH_AZ * dates_here + a * dates_here
                lines.append(jnp.concatenate([re, x[start : start + dates_here]], axis=0))
            for j, window in enumerate(block_transpose(lines, PATCH_RG)):
                z_ref[c * per_half + j, pl.ds(s * dates_here, dates_here), :] = window[:dates_here]
                z_ref[c * per_half + j, pl.ds(total + s * dates_here, dates_here), :] = window[dates_here:]
    windows = halves * per_half
    together = 2

    def step(i, carry):
        for q in range(together):
            w = i * together + q
            z_ref[w] = whiten_window(z_ref[w].astype(jnp.bfloat16))
        return carry

    lax.fori_loop(0, windows // together, step, 0)
    chunk = 16

    def back(r, carry):
        at = pl.ds(pl.multiple_of(r * chunk, chunk), chunk)
        for c in range(halves):
            lines = block_transpose([z_ref[c * per_half + j, at, :] for j in range(per_half)], PATCH_RG)
            for a in range(PATCH_AZ):
                tiles_ref[a * halves + c, at, :] = lines[a].astype(jnp.bfloat16)
        return carry

    lax.fori_loop(0, 2 * total // chunk, back, 0)

    def pack(o, carry):
        for i in range(CAP):
            out_ref[o, i] = tiles_ref[table_ref[o * CAP + i]]
        return carry

    lax.fori_loop(0, n, pack, 0)


def resample_kernel_body(slots, slot_ref, shift_ref, corr_ref, kern_ref, x_ref, out_ref, den_ref):
    row = lax.broadcasted_iota(jnp.int32, (TILE, TILE), 0)
    column = lax.broadcasted_iota(jnp.int32, (TILE, TILE), 1)
    apart = row - column + TILE
    for m in range(MAP_DEV):
        out_ref[m] = jnp.zeros(out_ref.shape[1:], jnp.float32)
        den_ref[m] = 0.0
    taps = [kern_ref[k] for k in range(KW)]

    def one(q):
        step = (apart - shift_ref[q]) & (TILE - 1)
        matrix = jnp.zeros((TILE, TILE), jnp.float32)
        for k in range(KW):
            matrix = jnp.where(step == k, taps[k], matrix)
        moved = jnp.dot(
            x_ref[q // CAP, q % CAP], matrix.astype(jnp.bfloat16), preferred_element_type=jnp.float32
        )
        weight = corr_ref[q].astype(jnp.float32)
        m = slot_ref[q]
        out_ref[m] += weight * moved
        den_ref[m] += weight

    def step(i, carry):
        for q in range(CAP):
            one(i * CAP + q)
        return carry

    lax.fori_loop(0, slots // CAP, step, 0)
    for m in range(MAP_DEV):
        out_ref[m] = out_ref[m] / jnp.maximum(den_ref[m], 1.0)


def shards(n, radar_stack, filter_taps, filter_lengths, resample_kernel, tile_owner, map_slot, correlation, offsets):
    dates_here, rows, ranges = radar_stack.shape[1:]
    dates = n * dates_here
    halves = ranges // TILE
    tile_count = tile_owner.shape[0]
    slots = n * CAP
    params = pltpu.CompilerParams(vmem_limit_bytes=BIG)

    owners = tile_owner[:, 0]
    tile_iota = jnp.arange(tile_count, dtype=jnp.int32)
    same = owners[:, None] == owners[None, :]
    rank = jnp.sum(jnp.logical_and(same, tile_iota[None, :] < tile_iota[:, None]), axis=1)
    slot_index = owners * CAP + rank
    placing = (jnp.arange(slots, dtype=jnp.int32)[:, None] == slot_index[None, :]).astype(jnp.int32)
    facts = jnp.stack([tile_iota, map_slot, offsets, correlation], axis=0)
    placed = jnp.sum(placing[None, :, :] * facts[:, None, :], axis=2)
    table = placed[0]
    details = jnp.pad(placed[1:].reshape(3, n, CAP).transpose(1, 0, 2), ((0, 0), (0, 5), (0, LANES - CAP)))

    cells = pl.pallas_call(
        partial(filter_kernel, n),
        out_shape=jax.ShapeDtypeStruct((n, halves, 2 * PATCH_AZ * dates_here, LANES), jnp.bfloat16),
        in_specs=[SMEM, VMEM, VMEM],
        out_specs=VMEM,
        scratch_shapes=[pltpu.VMEM((halves, n, 2 * PATCH_AZ * dates_here, LANES), jnp.float32)],
        compiler_params=params,
        name="filter",
    )(filter_lengths, radar_stack, filter_taps)
    got_cells, got_details = exchange(n, 0, cells, details)
    packed = pl.pallas_call(
        partial(whiten_kernel, n),
        out_shape=jax.ShapeDtypeStruct((n, CAP, 2 * dates, TILE), jnp.bfloat16),
        in_specs=[SMEM, VMEM],
        out_specs=VMEM,
        scratch_shapes=[
            pltpu.VMEM((ranges // PATCH_RG, 2 * dates, LANES), jnp.float32),
            pltpu.VMEM((tile_count, 2 * dates, TILE), jnp.bfloat16),
        ],
        compiler_params=params,
        name="whiten",
    )(table, got_cells)
    (got_tiles,) = exchange(n, 1, packed)
    arrived = got_details[:, :3, :CAP].transpose(1, 0, 2).reshape(3, slots)
    return pl.pallas_call(
        partial(resample_kernel_body, slots),
        out_shape=jax.ShapeDtypeStruct((MAP_DEV, 2 * dates, TILE), jnp.float32),
        in_specs=[SMEM, SMEM, SMEM, SMEM, VMEM],
        out_specs=VMEM,
        scratch_shapes=[pltpu.SMEM((MAP_DEV,), jnp.float32)],
        compiler_params=params,
        name="resample",
    )(arrived[0], arrived[1], arrived[2], resample_kernel, got_tiles)


def solution(mesh):
    in_specs = (
        P(None, "date", "grp", None),
        P(None, "date", None),
        P("date"),
        P(),
        P(("grp", "date"), None),
        P(("grp", "date")),
        P(("grp", "date")),
        P(("grp", "date")),
    )
    out_specs = P(("grp", "date"), None, None)
    return jax.shard_map(
        partial(shards, mesh.shape["date"]), mesh=mesh, in_specs=in_specs, out_specs=out_specs, check_vma=False
    )
```

profile of v0, /device:TPU:13, one launch (start us, length us, event | category | flops | bytes accessed | tf_op | source)
XLA Modules:
  0.0 128.5 jit_solution(15498257162485028368)
XLA Ops:
  0.0 0.9 convert_reduce_fusion
  0.9 0.7 multiply_add_fusion
  1.6 0.7 pad_add_fusion
  2.3 0.1 fusion
  2.3 0.1 multiply_reduce_fusion
  2.4 0.6 slice_bitcast_fusion.1.table_ref
  3.0 0.1 reshape.41
  3.1 0.6 pad.4.refs_1_
  3.8 2.9 %filter.1.refs_0_ = bf16[16,2,128,128]{3,2,1,0:T(8,128)(2,1)} custom-call(s32[8]{0:T(128)} %len_ref.1, bf16[2,8,128,256]{3,2,1,0:T(8,128)(2,1)} %radar_ref.1, f32[2,8,128]{2,1,0:T(8,128)} %taps_ref.1), custom_call_target="tpu_custom_call" | custom-call | tf_op jit(solution)/shard_map/filter/pallas_call | solution.py:279
  6.7 31.8 %exchange0.1 = (bf16[16,2,128,128]{3,2,1,0:T(8,128)(2,1)}, s32[16,8,128]{2,1,0:T(8,128)}) custom-call(bf16[16,2,128,128]{3,2,1,0:T(8,128)(2,1)} %filter.1.refs_0_, s32[16,8,128]{2,1,0:T(8,128)} %pad.4.refs_1_), custom_call_target="tpu_custom_call" | custom-call | tf_op jit(solution)/shard_map/exchange0/pallas_call | solution.py:130
  38.5 0.8 slice_bitcast_fusion
  39.3 0.1 slice_reduce_fusion
  39.4 0.7 squeeze.18.corr_ref
  40.1 0.6 squeeze.17.shift_ref
  40.7 0.6 squeeze.16.slot_ref
  41.3 28.5 %whiten.1.refs_0_ = bf16[16,2,256,128]{3,2,1,0:T(8,128)(2,1)} custom-call(s32[32]{0:T(128)} %slice_bitcast_fusion.1.table_ref, bf16[16,2,128,128]{3,2,1,0:T(8,128)(2,1)} %get-tuple-element.8.x_ref), custom_call_target="tpu_custom_call" | custom-call | tf_op jit(solution)/shard_map/whiten/pallas_call | solution.py:289
  69.8 52.4 %exchange1.1.x_ref = bf16[16,2,256,128]{3,2,1,0:T(8,128)(2,1)} custom-call(bf16[16,2,256,128]{3,2,1,0:T(8,128)(2,1)} %whiten.1.refs_0_), custom_call_target="tpu_custom_call" | custom-call | tf_op jit(solution)/shard_map/exchange1/pallas_call | solution.py:130
  122.3 6.2 %resample.1 = f32[8,256,128]{2,1,0:T(8,128)} custom-call(s32[32]{0:T(128)} %squeeze.16.slot_ref, s32[32]{0:T(128)} %squeeze.17.shift_ref, s32[32]{0:T(128)} %squeeze.18.corr_ref, f32[4]{0:T(128)} %kern_ref.1, bf16[16,2,256,128]{3,2,1,0:T(8,128)(2,1)} %exchange1.1.x_ref), custom_call_target="tpu_custom_call" | custom-call | tf_op jit(solution)/shard_map/resample/pallas_call | solution.py:303
  (3 shorter events, 0.0 us)
where the time goes:
time: 129 us; the launch traced here: 128 us
  Pallas kernels  122 us (95%)
  local copies, waits for them, and re-layouts  4.14 us (3%)
  other arithmetic  2.43 us (2%)
    pallas_call x2, Pallas kernels, exchange(): pl.pallas_call(partial(exchange_kernel, n, count), out_shape=[jax.ShapeDt...  84.2 us
    pallas_call x1, Pallas kernels, shards(): pl.pallas_call(partial(whiten_kernel, n), out_shape=jax.ShapeDtypeStruct(...  28.5 us
    pallas_call x1, Pallas kernels, shards(): pl.pallas_call(partial(resample_kernel_body, slots), out_shape=jax.ShapeD...  6.19 us
    pallas_call x1, Pallas kernels, shards(): pl.pallas_call(partial(filter_kernel, n), out_shape=jax.ShapeDtypeStruct(...  2.92 us

commit v1 on v0

v1 whole, which is shorter than its diff:
```python
from functools import partial

import jax
import jax.numpy as jnp
from jax import lax
from jax.experimental import pallas as pl
from jax.experimental.pallas import tpu as pltpu
from jax.sharding import PartitionSpec as P

PATCH_AZ = 8
PATCH_RG = 16
TILE = 128
KW = 4
CAP = 2
MAP_DEV = 8
LANES = 128
PHASES = 2
TOGETHER = 2

diag_load = 0.5
small_eps = 1e-05
MESH = pl.DeviceIdType.MESH
VMEM = pl.BlockSpec(memory_space=pltpu.VMEM)
SMEM = pl.BlockSpec(memory_space=pltpu.SMEM)
BIG = 60 * 1024 * 1024


def block_transpose(parts, group):
    count = len(parts)
    lane = lax.broadcasted_iota(jnp.int32, parts[0].shape, 1) // group
    bit = 1
    while bit < count:
        low = (lane // bit) % 2 == 0
        new = list(parts)
        for a in range(count):
            if a & bit == 0:
                x, y = parts[a], parts[a | bit]
                new[a] = jnp.where(low, x, pltpu.roll(y, bit * group, 1))
                new[a | bit] = jnp.where(low, pltpu.roll(x, LANES - bit * group, 1), y)
        parts = new
        bit *= 2
    return parts


def filter_kernel(n, len_ref, owner_ref, radar_ref, taps_ref, *refs):
    fact_refs, (out_ref, facts_ref, table_ref, rows_ref, seen_ref) = refs[:4], refs[4:]
    dates, rows = radar_ref.shape[1], radar_ref.shape[2]
    taps = taps_ref.shape[2]
    tile_count = owner_ref.shape[0]
    half = LANES // PHASES

    facts_ref[...] = jnp.full(facts_ref.shape, -1, jnp.int32)
    for i, fact in enumerate(fact_refs):
        facts_ref[pl.ds(i, 1), pl.ds(0, tile_count)] = fact[...]
    for o in range(n):
        seen_ref[o] = 0
        for i in range(CAP):
            table_ref[o * CAP + i] = 0
    for t in range(tile_count):
        owner = owner_ref[t]
        rank = seen_ref[owner]
        table_ref[owner * CAP + rank] = t
        seen_ref[owner] = rank + 1

    position = lax.broadcasted_iota(jnp.int32, (1, taps), 1)
    a_iota = lax.broadcasted_iota(jnp.int32, (rows, rows), 0)
    b_iota = lax.broadcasted_iota(jnp.int32, (rows, rows), 1)
    at = b_iota - a_iota + taps // 2
    inside = jnp.logical_and(at >= 0, at < taps)
    low = lax.broadcasted_iota(jnp.int32, (2 * rows, LANES), 1) < half
    for d in range(dates):

        def toeplitz(which):
            h = jnp.where(position < len_ref[d], taps_ref[which, pl.ds(d, 1), :], 0.0)
            wide = jnp.broadcast_to(h, (rows, taps))
            rolled = pltpu.roll(wide, taps // 2, 1, stride=1, stride_axis=0)
            full = jnp.concatenate([rolled] * (rows // taps), axis=1)
            return jnp.where(inside, full, 0.0)

        t_re, t_im = toeplitz(0), toeplitz(1)
        operator = jnp.concatenate(
            [jnp.concatenate([t_re, -t_im], axis=1), jnp.concatenate([t_im, t_re], axis=1)], axis=0
        ).astype(jnp.bfloat16)
        columns = jnp.concatenate([radar_ref[0, d], radar_ref[1, d]], axis=0)
        product = jnp.dot(operator, columns, preferred_element_type=jnp.float32)
        left, right = product[:, :LANES], product[:, LANES:]
        phases = (
            jnp.where(low, left, pltpu.roll(right, half, 1)),
            jnp.where(low, pltpu.roll(left, half, 1), right),
        )
        for h, phase in enumerate(phases):
            for p in range(n):
                for part in range(2):
                    top = part * rows + p * PATCH_AZ
                    rows_ref[h, p, pl.ds(part * PATCH_AZ * dates + d, PATCH_AZ, stride=dates), :] = phase[
                        top : top + PATCH_AZ
                    ]
    for h in range(PHASES):
        for p in range(n):
            out_ref[h, p] = rows_ref[h, p].astype(jnp.bfloat16)


def whiten_window(z):
    dates, looks = z.shape[0] // 2, z.shape[1]
    gram = lax.dot_general(z, z, (((1,), (1,)), ((), ())), preferred_element_type=jnp.float32)
    gram_re = (gram[:dates, :dates] + gram[dates:, dates:]) * (1.0 / looks)
    gram_im = (gram[dates:, :dates] - gram[:dates, dates:]) * (1.0 / looks)
    eye = lax.broadcasted_iota(jnp.int32, (dates, dates), 0) == lax.broadcasted_iota(
        jnp.int32, (dates, dates), 1
    )
    diagonal = jnp.where(eye, gram_re, 0.0)
    scale_col = lax.rsqrt(jnp.sum(diagonal, axis=1, keepdims=True) + small_eps)
    scale_row = lax.rsqrt(jnp.sum(diagonal, axis=0, keepdims=True) + small_eps)
    outer = scale_col * scale_row
    coher_re = gram_re * outer + jnp.where(eye, diag_load, 0.0)
    coher_im = gram_im * outer
    sums = jnp.sum(jnp.abs(coher_re) + jnp.abs(coher_im), axis=1, keepdims=True)
    over = 1.0 / jnp.max(sums, axis=0, keepdims=True)

    def embed(re, im):
        re, im = re.astype(jnp.bfloat16), im.astype(jnp.bfloat16)
        top = jnp.concatenate([re, -im], axis=1)
        return top, jnp.concatenate([top, jnp.concatenate([im, re], axis=1)], axis=0)

    part_re, part_im = coher_re * over, coher_im * over
    stages = []
    for stage in range(3):
        top, whole = embed(part_re, part_im)
        stages.append(whole)
        if stage < 2:
            square = jnp.dot(top, whole, preferred_element_type=jnp.float32)
            part_re = 2.0 * part_re - square[:, :dates]
            part_im = 2.0 * part_im + square[:, dates:]
    w = z.astype(jnp.float32)
    for whole in reversed(stages):
        w = 2.0 * w - jnp.dot(whole, w.astype(jnp.bfloat16), preferred_element_type=jnp.float32)
    return w * over


def flow_kernel(n, table_ref, kern_ref, cells_ref, facts_ref, *refs):
    total_ref, den_ref, got_cells, got_facts, z_ref, tiles_ref, out_msg, got_msg = refs[:8]
    own_sem, fact_send, fact_recv, cell_send, cell_recv, msg_send, msg_recv = refs[8:]
    me = lax.axis_index("date")
    rows = cells_ref.shape[2]
    dates_here = rows // (2 * PATCH_AZ)
    total = n * dates_here
    half = LANES // PHASES
    windows = LANES // PATCH_RG

    barrier = pltpu.get_barrier_semaphore()
    for k in range(1, n):
        pl.semaphore_signal(barrier, inc=1, device_id={"date": lax.rem(me + k, n)}, device_id_type=MESH)
    own = [pltpu.make_async_copy(cells_ref.at[h, me], got_cells.at[h, me], own_sem.at[h]) for h in range(PHASES)]
    own.append(pltpu.make_async_copy(facts_ref, got_facts.at[me], own_sem.at[PHASES]))
    for copy in own:
        copy.start()
    pl.semaphore_wait(barrier, n - 1)

    def remote(src, dst, send, recv, peer):
        return pltpu.make_async_remote_copy(
            src_ref=src, dst_ref=dst, send_sem=send, recv_sem=recv, device_id={"date": peer}, device_id_type=MESH
        )

    def fact_copy(peer, origin):
        return remote(facts_ref, got_facts.at[origin], fact_send.at[peer], fact_recv.at[origin], peer)

    def cell_copy(h, peer, origin):
        return remote(
            cells_ref.at[h, peer], got_cells.at[h, origin], cell_send.at[h, peer], cell_recv.at[h, origin], peer
        )

    def msg_copy(h, peer, origin):
        return remote(
            out_msg.at[h, peer], got_msg.at[h, origin], msg_send.at[h, peer], msg_recv.at[h, origin], peer
        )

    def after(k):
        return lax.rem(me + k, n)

    def before(k):
        return lax.rem(me + n - k, n)

    for h in range(PHASES):
        for k in range(1, n):
            cell_copy(h, after(k), me).start()
        if h == 0:
            for k in range(1, n):
                fact_copy(after(k), me).start()

    low = lax.broadcasted_iota(jnp.int32, (2 * total, LANES), 1) < half
    for h in range(PHASES):
        own[h].wait()
        for k in range(1, n):
            cell_copy(h, before(k), before(k)).wait_recv()
        for s in range(n):
            x = got_cells[h, s].astype(jnp.float32)
            lines = []
            for a in range(PATCH_AZ):
                re = x[a * dates_here : (a + 1) * dates_here]
                start = (PATCH_AZ + a) * dates_here
                lines.append(jnp.concatenate([re, x[start : start + dates_here]], axis=0))
            for j, window in enumerate(block_transpose(lines, PATCH_RG)):
                z_ref[j, pl.ds(s * dates_here, dates_here), :] = window[:dates_here]
                z_ref[j, pl.ds(total + s * dates_here, dates_here), :] = window[dates_here:]

        def whiten(i, carry):
            for q in range(TOGETHER):
                z_ref[i * TOGETHER + q] = whiten_window(z_ref[i * TOGETHER + q].astype(jnp.bfloat16))
            return carry

        lax.fori_loop(0, windows // TOGETHER, whiten, 0)
        chunk = 16

        def back(r, carry):
            at = pl.ds(pl.multiple_of(r * chunk, chunk), chunk)
            first = lax.broadcasted_iota(jnp.int32, (chunk, LANES), 1) < half
            lines = block_transpose([z_ref[j, at, :] for j in range(windows)], PATCH_RG)
            for a in range(PATCH_AZ):
                turned = pltpu.roll(lines[a], half, 1)
                tiles_ref[a * 2, at, :] = jnp.where(first, lines[a], turned).astype(jnp.bfloat16)
                tiles_ref[a * 2 + 1, at, :] = jnp.where(first, turned, lines[a]).astype(jnp.bfloat16)
            return carry

        lax.fori_loop(0, 2 * total // chunk, back, 0)

        def message(o):
            return jnp.where(low, tiles_ref[table_ref[o * CAP]], tiles_ref[table_ref[o * CAP + 1]])

        def pack(k, carry):
            o = after(k)
            out_msg[h, o] = message(o)
            return carry

        lax.fori_loop(1, n, pack, 0)
        got_msg[h, me] = message(me)
        for k in range(1, n):
            msg_copy(h, after(k), me).start()

    total_ref[...] = jnp.zeros(total_ref.shape, jnp.float32)
    den_ref[...] = jnp.zeros(den_ref.shape, jnp.float32)
    apart = lax.broadcasted_iota(jnp.int32, (TILE, TILE), 0) - lax.broadcasted_iota(jnp.int32, (TILE, TILE), 1) + TILE
    lane = lax.broadcasted_iota(jnp.int32, (1, LANES), 1)
    map_row = lax.broadcasted_iota(jnp.int32, den_ref.shape, 0)
    blank = jnp.zeros((half, TILE), jnp.bfloat16)

    def gather(s):
        facts = got_facts[s].astype(jnp.float32)
        mine = got_facts[s, pl.ds(0, 1), :] == me
        place = lane.astype(jnp.float32)
        first = jnp.min(jnp.where(mine, place, 2.0 * LANES), axis=1, keepdims=True)
        last = jnp.max(jnp.where(mine, place, -1.0), axis=1, keepdims=True)
        columns, weights = [], []
        for i, at in enumerate((first, last)):
            picked = jnp.sum(jnp.where(place == at, facts, 0.0), axis=1, keepdims=True)
            slot, shift, corr = picked[1:2], picked[2:3].astype(jnp.int32), picked[3:4]
            if i:
                corr = jnp.where(last > first, corr, 0.0)
            step = (apart - shift) & (TILE - 1)
            circ = jnp.zeros((TILE, TILE), jnp.float32)
            for k in range(KW):
                circ = jnp.where(step == k, kern_ref[k], circ)
            circ = circ.astype(jnp.bfloat16)
            pieces = [circ[:half], blank, circ[half:], blank] if i == 0 else [blank, circ[:half], blank, circ[half:]]
            columns.append(jnp.concatenate(pieces, axis=0))
            weights.append(jnp.where(map_row == slot.astype(jnp.int32), corr, 0.0))
        x = jnp.concatenate([got_msg[h, s] for h in range(PHASES)], axis=1)
        moved = jnp.dot(x, jnp.concatenate(columns, axis=1), preferred_element_type=jnp.float32)
        den_ref[...] += weights[0] + weights[1]
        for m in range(MAP_DEV):
            total_ref[m] += (
                weights[0][m : m + 1] * moved[:, :TILE] + weights[1][m : m + 1] * moved[:, TILE:]
            )

    own[PHASES].wait()
    gather(me)

    def arrive(k, carry):
        s = before(k)
        fact_copy(s, s).wait_recv()
        for h in range(PHASES):
            msg_copy(h, s, s).wait_recv()
        gather(s)
        return carry

    lax.fori_loop(1, n, arrive, 0)
    for k in range(1, n):
        fact_copy(after(k), me).wait_send()
        for h in range(PHASES):
            cell_copy(h, after(k), me).wait_send()
            msg_copy(h, after(k), me).wait_send()


def shards(n, radar_stack, filter_taps, filter_lengths, resample_kernel, tile_owner, map_slot, correlation, offsets):
    dates_here, rows, ranges = radar_stack.shape[1:]
    dates = n * dates_here
    tile_count = tile_owner.shape[0]
    block = (PHASES, n, 2 * PATCH_AZ * dates_here, LANES)
    message = (PHASES, n, 2 * dates, LANES)
    facts = [x.reshape(1, tile_count) for x in (tile_owner, map_slot, offsets, correlation)]

    cells, known, table = pl.pallas_call(
        partial(filter_kernel, n),
        out_shape=[
            jax.ShapeDtypeStruct(block, jnp.bfloat16),
            jax.ShapeDtypeStruct((8, LANES), jnp.int32),
            jax.ShapeDtypeStruct((n * CAP,), jnp.int32),
        ],
        in_specs=[SMEM, SMEM] + [VMEM] * 6,
        out_specs=[VMEM, VMEM, SMEM],
        scratch_shapes=[pltpu.VMEM(block, jnp.float32), pltpu.SMEM((n,), jnp.int32)],
        compiler_params=pltpu.CompilerParams(vmem_limit_bytes=BIG),
        name="filter",
    )(filter_lengths, tile_owner.reshape(tile_count), radar_stack, filter_taps, *facts)
    dma = pltpu.SemaphoreType.DMA
    total, den = pl.pallas_call(
        partial(flow_kernel, n),
        out_shape=[
            jax.ShapeDtypeStruct((MAP_DEV, 2 * dates, TILE), jnp.float32),
            jax.ShapeDtypeStruct((MAP_DEV, TILE), jnp.float32),
        ],
        in_specs=[SMEM, SMEM, VMEM, VMEM],
        out_specs=[VMEM, VMEM],
        scratch_shapes=[
            pltpu.VMEM(block, jnp.bfloat16),
            pltpu.VMEM((n, 8, LANES), jnp.int32),
            pltpu.VMEM((LANES // PATCH_RG, 2 * dates, LANES), jnp.float32),
            pltpu.VMEM((tile_count, 2 * dates, LANES), jnp.bfloat16),
            pltpu.VMEM(message, jnp.bfloat16),
            pltpu.VMEM(message, jnp.bfloat16),
            dma((PHASES + 1,)),
            dma((n,)),
            dma((n,)),
            dma((PHASES, n)),
            dma((PHASES, n)),
            dma((PHASES, n)),
            dma((PHASES, n)),
        ],
        compiler_params=pltpu.CompilerParams(collective_id=0, has_side_effects=True, vmem_limit_bytes=BIG),
        name="flow",
    )(table, resample_kernel, cells, known)
    return total / jnp.maximum(den[:, :1, None], 1.0)


def solution(mesh):
    in_specs = (
        P(None, "date", "grp", None),
        P(None, "date", None),
        P("date"),
        P(),
        P(("grp", "date"), None),
        P(("grp", "date")),
        P(("grp", "date")),
        P(("grp", "date")),
    )
    out_specs = P(("grp", "date"), None, None)
    return jax.shard_map(
        partial(shards, mesh.shape["date"]), mesh=mesh, in_specs=in_specs, out_specs=out_specs, check_vma=False
    )
```

time: 129 us -> 98.6 us (0.76)
  the two profiles are of different devices: /device:TPU:13 before, /device:TPU:31 now
where the time goes in v1:
time: 98.6 us; the launch traced here: 98.4 us
  Pallas kernels  95.2 us (97%)
  other arithmetic  3.14 us (3%)
    pallas_call x1, Pallas kernels, shards(): pl.pallas_call(partial(flow_kernel, n), out_shape=[jax.ShapeDtypeStruct((...  91.4 us
    pallas_call x1, Pallas kernels, shards(): pl.pallas_call(partial(filter_kernel, n), out_shape=[jax.ShapeDtypeStruct...  3.86 us
    div x1, other arithmetic, shards(): return total / jnp.maximum(den[:, :1, None], 1.0)  2.35 us

profile of v1, /device:TPU:31, one launch (start us, length us, event | category | flops | bytes accessed | tf_op | source)
XLA Modules:
  0.0 98.4 jit_solution(7326005525545824680)
XLA Ops:
  0.0 3.9 %filter.1 = (bf16[2,16,128,128]{3,2,1,0:T(8,128)(2,1)}, s32[8,128]{1,0:T(8,128)}, s32[32]{0:T(128)}) custom-call(s32[8]{0:T(128)} %len_ref.1, s32[16]{0:T(128)} %bitcast.5, bf16[2,8,128,256]{3,2,1,0:T(8,128)(2,1)} %radar_ref.1, f32[2,8,128]{2,1,0:T(8,128)} %taps_ref.1, s32[1,16]{1,0:T(1,128)} %bitcast.6, s32[1,16]{1,0:T(1,128)} %bitcast.7, s32[1,16]{1,0:T(1,128)} %bitcast.8, ...), custom_call_target="tpu_custom_call" | custom-call | tf_op jit(solution)/shard_map/filter/pallas_call | solution.py:301
  3.9 91.4 %flow.1 = (f32[8,256,128]{2,1,0:T(8,128)}, f32[8,128]{1,0:T(8,128)}) custom-call(s32[32]{0:T(128)} %get-tuple-element.10.table_ref, f32[4]{0:T(128)} %kern_ref.1, bf16[2,16,128,128]{3,2,1,0:T(8,128)(2,1)} %get-tuple-element.11.cells_ref, s32[8,128]{1,0:T(8,128)} %get-tuple-element.12.facts_ref), custom_call_target="tpu_custom_call" | custom-call | tf_op jit(solution)/shard_map/flow/pallas_call | solution.py:315
  95.3 0.8 maximum_reduce_fusion
  96.0 2.3 %broadcast_divide_fusion = f32[8,256,128]{2,1,0:T(8,128)} fusion(f32[8,256,128]{2,1,0:T(8,128)} %get-tuple-element.13, f32[8]{0:T(128)S(1)} %maximum_reduce_fusion), kind=kLoop, calls=%fused_computation | loop fusion | flops 262144 | bytes 2097184 | tf_op jit(solution)/shard_map/div | solution.py:341

commit v2 on v1

v2 whole, which is shorter than its diff:
```python
from functools import partial

import jax
import jax.numpy as jnp
from jax import lax
from jax.experimental import pallas as pl
from jax.experimental.pallas import tpu as pltpu
from jax.sharding import PartitionSpec as P

PATCH_AZ = 8
PATCH_RG = 16
TILE = 128
KW = 4
CAP = 2
MAP_DEV = 8
LANES = 128
PHASES = 2
TOGETHER = 4
SWEEPS = 3

diag_load = 0.5
small_eps = 1e-05
MESH = pl.DeviceIdType.MESH
VMEM = pl.BlockSpec(memory_space=pltpu.VMEM)
SMEM = pl.BlockSpec(memory_space=pltpu.SMEM)
BIG = 60 * 1024 * 1024


def filter_kernel(n, len_ref, owner_ref, radar_ref, taps_ref, *refs):
    fact_refs, (out_ref, facts_ref, table_ref, rows_ref, seen_ref) = refs[:4], refs[4:]
    dates, rows = radar_ref.shape[1], radar_ref.shape[2]
    taps = taps_ref.shape[2]
    tile_count = owner_ref.shape[0]
    half = LANES // PHASES

    facts_ref[...] = jnp.full(facts_ref.shape, -1, jnp.int32)
    for i, fact in enumerate(fact_refs):
        facts_ref[pl.ds(i, 1), pl.ds(0, tile_count)] = fact[...]
    for o in range(n):
        seen_ref[o] = 0
        for i in range(CAP):
            table_ref[o * CAP + i] = 0
    for t in range(tile_count):
        owner = owner_ref[t]
        rank = seen_ref[owner]
        table_ref[owner * CAP + rank] = t
        seen_ref[owner] = rank + 1

    position = lax.broadcasted_iota(jnp.int32, (1, taps), 1)
    a_iota = lax.broadcasted_iota(jnp.int32, (rows, rows), 0)
    b_iota = lax.broadcasted_iota(jnp.int32, (rows, rows), 1)
    at = b_iota - a_iota + taps // 2
    inside = jnp.logical_and(at >= 0, at < taps)
    low = lax.broadcasted_iota(jnp.int32, (2 * rows, LANES), 1) < half
    for d in range(dates):

        def toeplitz(which):
            h = jnp.where(position < len_ref[d], taps_ref[which, pl.ds(d, 1), :], 0.0)
            wide = jnp.broadcast_to(h, (rows, taps))
            rolled = pltpu.roll(wide, taps // 2, 1, stride=1, stride_axis=0)
            full = jnp.concatenate([rolled] * (rows // taps), axis=1)
            return jnp.where(inside, full, 0.0)

        t_re, t_im = toeplitz(0), toeplitz(1)
        operator = jnp.concatenate(
            [jnp.concatenate([t_re, -t_im], axis=1), jnp.concatenate([t_im, t_re], axis=1)], axis=0
        ).astype(jnp.bfloat16)
        columns = jnp.concatenate([radar_ref[0, d], radar_ref[1, d]], axis=0)
        product = jnp.dot(operator, columns, preferred_element_type=jnp.float32)
        left, right = product[:, :LANES], product[:, LANES:]
        phases = (
            jnp.where(low, left, pltpu.roll(right, half, 1)),
            jnp.where(low, pltpu.roll(left, half, 1), right),
        )
        for h, phase in enumerate(phases):
            for p in range(n):
                for part in range(2):
                    top = part * rows + p * PATCH_AZ
                    rows_ref[h, p, pl.ds(part * PATCH_AZ * dates + d, PATCH_AZ, stride=dates), :] = phase[
                        top : top + PATCH_AZ
                    ]
    for h in range(PHASES):
        for p in range(n):
            out_ref[h, p] = rows_ref[h, p].astype(jnp.bfloat16)


def whiten_window(zt):
    looks, dates = zt.shape[0], zt.shape[1] // 2
    gram = lax.dot_general(zt, zt, (((0,), (0,)), ((), ())), preferred_element_type=jnp.float32)
    gram_re = (gram[:dates, :dates] + gram[dates:, dates:]) * (1.0 / looks)
    gram_im = (gram[dates:, :dates] - gram[:dates, dates:]) * (1.0 / looks)
    eye = lax.broadcasted_iota(jnp.int32, (dates, dates), 0) == lax.broadcasted_iota(
        jnp.int32, (dates, dates), 1
    )
    diagonal = jnp.where(eye, gram_re, 0.0)
    scale_col = lax.rsqrt(jnp.sum(diagonal, axis=1, keepdims=True) + small_eps)
    scale_row = lax.rsqrt(jnp.sum(diagonal, axis=0, keepdims=True) + small_eps)
    outer = scale_col * scale_row
    coher_re = gram_re * outer + jnp.where(eye, diag_load, 0.0)
    coher_im = gram_im * outer
    sums = jnp.sum(jnp.abs(coher_re) + jnp.abs(coher_im), axis=1, keepdims=True)
    over = 1.0 / jnp.max(sums, axis=0, keepdims=True)

    part_re, part_im = coher_re * over, coher_im * over
    w, rounded = zt.astype(jnp.float32), zt
    for stage in range(SWEEPS):
        re, im = part_re.astype(jnp.bfloat16), part_im.astype(jnp.bfloat16)
        top = jnp.concatenate([re, -im], axis=1)
        whole = jnp.concatenate([top, jnp.concatenate([im, re], axis=1)], axis=0)
        if stage < SWEEPS - 1:
            both = jnp.dot(jnp.concatenate([top, rounded], axis=0), whole, preferred_element_type=jnp.float32)
            part_re = 2.0 * part_re - both[:dates, :dates]
            part_im = 2.0 * part_im + both[:dates, dates:]
            applied = both[dates:]
        else:
            applied = jnp.dot(rounded, whole, preferred_element_type=jnp.float32)
        w = 2.0 * w - applied
        rounded = w.astype(jnp.bfloat16)
    return (w * over).astype(jnp.bfloat16)


def flow_kernel(n, table_ref, kern_ref, cells_ref, facts_ref, *refs):
    result_ref, got_cells, got_facts, cell_ref, z_ref, tiles_ref, out_msg, got_msg, total_ref, den_ref = refs[:10]
    own_sem, fact_send, fact_recv, cell_send, cell_recv, msg_send, msg_recv = refs[10:]
    me = lax.axis_index("date")
    rows = cells_ref.shape[2]
    dates_here = rows // (2 * PATCH_AZ)
    total = n * dates_here
    half = LANES // PHASES
    windows = LANES // PATCH_RG

    barrier = pltpu.get_barrier_semaphore()
    for k in range(1, n):
        pl.semaphore_signal(barrier, inc=1, device_id={"date": lax.rem(me + k, n)}, device_id_type=MESH)
    own = [pltpu.make_async_copy(cells_ref.at[h, me], got_cells.at[h, me], own_sem.at[h]) for h in range(PHASES)]
    own.append(pltpu.make_async_copy(facts_ref, got_facts.at[me], own_sem.at[PHASES]))
    for copy in own:
        copy.start()
    pl.semaphore_wait(barrier, n - 1)

    def remote(src, dst, send, recv, peer):
        return pltpu.make_async_remote_copy(
            src_ref=src, dst_ref=dst, send_sem=send, recv_sem=recv, device_id={"date": peer}, device_id_type=MESH
        )

    def fact_copy(peer, origin):
        return remote(facts_ref, got_facts.at[origin], fact_send.at[peer], fact_recv.at[origin], peer)

    def cell_copy(h, peer, origin):
        return remote(
            cells_ref.at[h, peer], got_cells.at[h, origin], cell_send.at[h, peer], cell_recv.at[h, origin], peer
        )

    def msg_copy(h, peer, origin):
        return remote(
            out_msg.at[h, peer], got_msg.at[h, origin], msg_send.at[h, peer], msg_recv.at[h, origin], peer
        )

    def partner(k):
        peer, bit = me, 1
        while bit < n:
            peer = peer + (k // bit) % 2 * (1 - (me // bit) % 2 * 2) * bit
            bit *= 2
        return peer

    far_first = range(n - 1, 0, -1)

    for h in range(PHASES):
        for k in far_first:
            cell_copy(h, partner(k), me).start()
        if h == 0:
            for k in far_first:
                fact_copy(partner(k), me).start()

    per_half = windows // 2
    for h in range(PHASES):
        own[h].wait()
        for k in far_first:
            cell_copy(h, partner(k), partner(k)).wait_recv()
        for s in range(n):
            cell_ref[s] = got_cells[h, s].astype(jnp.float32)
        for part in range(2):
            for a in range(PATCH_AZ):
                at = pl.ds((part * PATCH_AZ + a) * dates_here, dates_here)
                line = jnp.concatenate([cell_ref[s, at, :] for s in range(n)], axis=0).T.astype(jnp.bfloat16)
                for j in range(windows):
                    z_ref[j, a * PATCH_RG : (a + 1) * PATCH_RG, part * total : (part + 1) * total] = line[
                        j * PATCH_RG : (j + 1) * PATCH_RG
                    ]

        def whiten(i, carry):
            for q in range(TOGETHER):
                side = i * TOGETHER // per_half
                j = i * TOGETHER % per_half + q
                white = whiten_window(z_ref[i * TOGETHER + q])
                for a in range(PATCH_AZ):
                    tiles_ref[a * 2 + side, pl.ds(j * PATCH_RG, PATCH_RG), :] = white[
                        a * PATCH_RG : (a + 1) * PATCH_RG
                    ]
            return carry

        lax.fori_loop(0, windows // TOGETHER, whiten, 0)

        def message(o, i):
            return tiles_ref[table_ref[o * CAP + i]]

        def pack(k, carry):
            o = partner(k)
            for i in range(CAP):
                out_msg[h, o, pl.ds(i * half, half), :] = message(o, i)
            return carry

        lax.fori_loop(1, n, pack, 0)
        for i in range(CAP):
            got_msg[h, me, pl.ds(i * half, half), :] = message(me, i)
        for k in far_first:
            msg_copy(h, partner(k), me).start()

    total_ref[...] = jnp.zeros(total_ref.shape, jnp.float32)
    den_ref[...] = jnp.zeros(den_ref.shape, jnp.float32)
    apart = lax.broadcasted_iota(jnp.int32, (TILE, TILE), 1) - lax.broadcasted_iota(jnp.int32, (TILE, TILE), 0) + TILE
    lane = lax.broadcasted_iota(jnp.int32, (1, LANES), 1)
    map_row = lax.broadcasted_iota(jnp.int32, den_ref.shape, 0)

    def gather(s):
        facts = got_facts[s].astype(jnp.float32)
        mine = got_facts[s, pl.ds(0, 1), :] == me
        place = lane.astype(jnp.float32)
        first = jnp.min(jnp.where(mine, place, 2.0 * LANES), axis=1, keepdims=True)
        last = jnp.max(jnp.where(mine, place, -1.0), axis=1, keepdims=True)
        moved, weights = [], []
        for i, at in enumerate((first, last)):
            picked = jnp.sum(jnp.where(place == at, facts, 0.0), axis=1, keepdims=True)
            slot, shift, corr = picked[1:2], picked[2:3].astype(jnp.int32), picked[3:4]
            if i:
                corr = jnp.where(last > first, corr, 0.0)
            step = (apart - shift) & (TILE - 1)
            circ = jnp.zeros((TILE, TILE), jnp.float32)
            for k in range(KW):
                circ = jnp.where(step == k, kern_ref[k], circ)
            x = jnp.concatenate([got_msg[h, s, pl.ds(i * half, half), :] for h in range(PHASES)], axis=0)
            moved.append(jnp.dot(circ.astype(jnp.bfloat16), x, preferred_element_type=jnp.float32))
            weights.append(jnp.where(map_row == slot.astype(jnp.int32), corr, 0.0))
        den_ref[...] += weights[0] + weights[1]
        for m in range(MAP_DEV):
            total_ref[m] += weights[0][m : m + 1, :1] * moved[0] + weights[1][m : m + 1, :1] * moved[1]

    own[PHASES].wait()
    gather(me)

    def arrive(i, carry):
        s = partner(n - i)
        fact_copy(s, s).wait_recv()
        for h in range(PHASES):
            msg_copy(h, s, s).wait_recv()
        gather(s)
        return carry

    lax.fori_loop(1, n, arrive, 0)
    for m in range(MAP_DEV):
        result_ref[m] = (total_ref[m] / jnp.maximum(den_ref[m : m + 1, :1], 1.0)).T
    for k in far_first:
        fact_copy(partner(k), me).wait_send()
        for h in range(PHASES):
            cell_copy(h, partner(k), me).wait_send()
            msg_copy(h, partner(k), me).wait_send()


def shards(n, radar_stack, filter_taps, filter_lengths, resample_kernel, tile_owner, map_slot, correlation, offsets):
    dates_here, rows, ranges = radar_stack.shape[1:]
    dates = n * dates_here
    tile_count = tile_owner.shape[0]
    block = (PHASES, n, 2 * PATCH_AZ * dates_here, LANES)
    message = (PHASES, n, LANES, 2 * dates)
    facts = [x.reshape(1, tile_count) for x in (tile_owner, map_slot, offsets, correlation)]

    cells, known, table = pl.pallas_call(
        partial(filter_kernel, n),
        out_shape=[
            jax.ShapeDtypeStruct(block, jnp.bfloat16),
            jax.ShapeDtypeStruct((8, LANES), jnp.int32),
            jax.ShapeDtypeStruct((n * CAP,), jnp.int32),
        ],
        in_specs=[SMEM, SMEM] + [VMEM] * 6,
        out_specs=[VMEM, VMEM, SMEM],
        scratch_shapes=[pltpu.VMEM(block, jnp.float32), pltpu.SMEM((n,), jnp.int32)],
        compiler_params=pltpu.CompilerParams(vmem_limit_bytes=BIG),
        name="filter",
    )(filter_lengths, tile_owner.reshape(tile_count), radar_stack, filter_taps, *facts)
    dma = pltpu.SemaphoreType.DMA
    return pl.pallas_call(
        partial(flow_kernel, n),
        out_shape=jax.ShapeDtypeStruct((MAP_DEV, 2 * dates, TILE), jnp.float32),
        in_specs=[SMEM, SMEM, VMEM, VMEM],
        out_specs=VMEM,
        scratch_shapes=[
            pltpu.VMEM(block, jnp.bfloat16),
            pltpu.VMEM((n, 8, LANES), jnp.int32),
            pltpu.VMEM(block[1:], jnp.float32),
            pltpu.VMEM((LANES // PATCH_RG, LANES, 2 * dates), jnp.bfloat16),
            pltpu.VMEM((tile_count, LANES // PHASES, 2 * dates), jnp.bfloat16),
            pltpu.VMEM(message, jnp.bfloat16),
            pltpu.VMEM(message, jnp.bfloat16),
            pltpu.VMEM((MAP_DEV, TILE, 2 * dates), jnp.float32),
            pltpu.VMEM((MAP_DEV, TILE), jnp.float32),
            dma((PHASES + 1,)),
            dma((n,)),
            dma((n,)),
            dma((PHASES, n)),
            dma((PHASES, n)),
            dma((PHASES, n)),
            dma((PHASES, n)),
        ],
        compiler_params=pltpu.CompilerParams(collective_id=0, has_side_effects=True, vmem_limit_bytes=BIG),
        name="flow",
    )(table, resample_kernel, cells, known)


def solution(mesh):
    in_specs = (
        P(None, "date", "grp", None),
        P(None, "date", None),
        P("date"),
        P(),
        P(("grp", "date"), None),
        P(("grp", "date")),
        P(("grp", "date")),
        P(("grp", "date")),
    )
    out_specs = P(("grp", "date"), None, None)
    return jax.shard_map(
        partial(shards, mesh.shape["date"]), mesh=mesh, in_specs=in_specs, out_specs=out_specs, check_vma=False
    )
```

time: 98.6 us -> 91.5 us (0.928)
  the two profiles are of different devices: /device:TPU:31 before, /device:TPU:0 now
where the time goes in v2:
time: 91.5 us; the launch traced here: 91.3 us
  Pallas kernels  89 us (97%)
  local copies, waits for them, and re-layouts  2.27 us (2%)
    pallas_call x1, Pallas kernels, shards(): pl.pallas_call(partial(flow_kernel, n), out_shape=jax.ShapeDtypeStruct((M...  85.1 us
    pallas_call x1, Pallas kernels, shards(): pl.pallas_call(partial(filter_kernel, n), out_shape=[jax.ShapeDtypeStruct...  3.86 us
    unnamed x1, local copies, waits for them, and re-layouts  2.27 us

profile of v2, /device:TPU:0, one launch (start us, length us, event | category | flops | bytes accessed | tf_op | source)
XLA Modules:
  0.0 91.3 jit_solution(3166459960722859115)
XLA Ops:
  0.0 3.9 %filter.1 = (bf16[2,16,128,128]{3,2,1,0:T(8,128)(2,1)}, s32[8,128]{1,0:T(8,128)}, s32[32]{0:T(128)}) custom-call(s32[8]{0:T(128)} %len_ref.1, s32[16]{0:T(128)} %bitcast.5, bf16[2,8,128,256]{3,2,1,0:T(8,128)(2,1)} %radar_ref.1, f32[2,8,128]{2,1,0:T(8,128)} %taps_ref.1, s32[1,16]{1,0:T(1,128)} %bitcast.6, s32[1,16]{1,0:T(1,128)} %bitcast.7, s32[1,16]{1,0:T(1,128)} %bitcast.8, ...), custom_call_target="tpu_custom_call" | custom-call | tf_op jit(solution)/shard_map/filter/pallas_call | solution.py:277
  3.9 85.1 %flow.1 = f32[8,256,128]{2,1,0:T(8,128)} custom-call(s32[32]{0:T(128)} %get-tuple-element.8.table_ref, f32[4]{0:T(128)} %kern_ref.1, bf16[2,16,128,128]{3,2,1,0:T(8,128)(2,1)} %get-tuple-element.9.cells_ref, s32[8,128]{1,0:T(8,128)} %get-tuple-element.10.facts_ref), custom_call_target="tpu_custom_call" | custom-call | tf_op jit(solution)/shard_map/flow/pallas_call | solution.py:291
  89.0 2.3 %copy.10 = f32[8,256,128]{2,1,0:T(8,128)} copy(f32[8,256,128]{2,1,0:T(8,128)} %flow.1) | data formatting | bytes 2097152

commit v3 on v2

--- a/solution.py
+++ b/solution.py
@@ -23,65 +23,7 @@
 MESH = pl.DeviceIdType.MESH
 VMEM = pl.BlockSpec(memory_space=pltpu.VMEM)
 SMEM = pl.BlockSpec(memory_space=pltpu.SMEM)
-BIG = 60 * 1024 * 1024
-
-
-def filter_kernel(n, len_ref, owner_ref, radar_ref, taps_ref, *refs):
-    fact_refs, (out_ref, facts_ref, table_ref, rows_ref, seen_ref) = refs[:4], refs[4:]
-    dates, rows = radar_ref.shape[1], radar_ref.shape[2]
-    taps = taps_ref.shape[2]
-    tile_count = owner_ref.shape[0]
-    half = LANES // PHASES
-
-    facts_ref[...] = jnp.full(facts_ref.shape, -1, jnp.int32)
-    for i, fact in enumerate(fact_refs):
-        facts_ref[pl.ds(i, 1), pl.ds(0, tile_count)] = fact[...]
-    for o in range(n):
-        seen_ref[o] = 0
-        for i in range(CAP):
-            table_ref[o * CAP + i] = 0
-    for t in range(tile_count):
-        owner = owner_ref[t]
-        rank = seen_ref[owner]
-        table_ref[owner * CAP + rank] = t
-        seen_ref[owner] = rank + 1
-
-    position = lax.broadcasted_iota(jnp.int32, (1, taps), 1)
-    a_iota = lax.broadcasted_iota(jnp.int32, (rows, rows), 0)
-    b_iota = lax.broadcasted_iota(jnp.int32, (rows, rows), 1)
-    at = b_iota - a_iota + taps // 2
-    inside = jnp.logical_and(at >= 0, at < taps)
-    low = lax.broadcasted_iota(jnp.int32, (2 * rows, LANES), 1) < half
-    for d in range(dates):
-
-        def toeplitz(which):
-            h = jnp.where(position < len_ref[d], taps_ref[which, pl.ds(d, 1), :], 0.0)
-            wide = jnp.broadcast_to(h, (rows, taps))
-            rolled = pltpu.roll(wide, taps // 2, 1, stride=1, stride_axis=0)
-            full = jnp.concatenate([rolled] * (rows // taps), axis=1)
-            return jnp.where(inside, full, 0.0)
-
-        t_re, t_im = toeplitz(0), toeplitz(1)
-        operator = jnp.concatenate(
-            [jnp.concatenate([t_re, -t_im], axis=1), jnp.concatenate([t_im, t_re], axis=1)], axis=0
-        ).astype(jnp.bfloat16)
-        columns = jnp.concatenate([radar_ref[0, d], radar_ref[1, d]], axis=0)
-        product = jnp.dot(operator, columns, preferred_element_type=jnp.float32)
-        left, right = product[:, :LANES], product[:, LANES:]
-        phases = (
-            jnp.where(low, left, pltpu.roll(right, half, 1)),
-            jnp.where(low, pltpu.roll(left, half, 1), right),
-        )
-        for h, phase in enumerate(phases):
-            for p in range(n):
-                for part in range(2):
-                    top = part * rows + p * PATCH_AZ
-                    rows_ref[h, p, pl.ds(part * PATCH_AZ * dates + d, PATCH_AZ, stride=dates), :] = phase[
-                        top : top + PATCH_AZ
-                    ]
-    for h in range(PHASES):
-        for p in range(n):
-            out_ref[h, p] = rows_ref[h, p].astype(jnp.bfloat16)
+BIG = 32 * 1024 * 1024
 
 
 def whiten_window(zt):
@@ -119,12 +61,14 @@
     return (w * over).astype(jnp.bfloat16)
 
 
-def flow_kernel(n, table_ref, kern_ref, cells_ref, facts_ref, *refs):
-    result_ref, got_cells, got_facts, cell_ref, z_ref, tiles_ref, out_msg, got_msg, total_ref, den_ref = refs[:10]
-    own_sem, fact_send, fact_recv, cell_send, cell_recv, msg_send, msg_recv = refs[10:]
+def flow_kernel(n, len_ref, owner_ref, kern_ref, radar_ref, taps_ref, *refs):
+    fact_refs, refs = refs[:4], refs[4:]
+    result_ref, cells_ref, got_cells, facts_ref, got_facts, cell_ref, z_ref, tiles_ref, out_msg, got_msg = refs[:10]
+    total_ref, den_ref, operator_ref, table_ref = refs[10:14]
+    own_sem, fact_send, fact_recv, cell_send, cell_recv, msg_send, msg_recv = refs[14:]
     me = lax.axis_index("date")
-    rows = cells_ref.shape[2]
-    dates_here = rows // (2 * PATCH_AZ)
+    dates_here, rows = radar_ref.shape[1], radar_ref.shape[2]
+    taps, tile_count = taps_ref.shape[2], owner_ref.shape[0]
     total = n * dates_here
     half = LANES // PHASES
     windows = LANES // PATCH_RG
@@ -134,9 +78,6 @@
         pl.semaphore_signal(barrier, inc=1, device_id={"date": lax.rem(me + k, n)}, device_id_type=MESH)
     own = [pltpu.make_async_copy(cells_ref.at[h, me], got_cells.at[h, me], own_sem.at[h]) for h in range(PHASES)]
     own.append(pltpu.make_async_copy(facts_ref, got_facts.at[me], own_sem.at[PHASES]))
-    for copy in own:
-        copy.start()
-    pl.semaphore_wait(barrier, n - 1)
 
     def remote(src, dst, send, recv, peer):
         return pltpu.make_async_remote_copy(
@@ -165,12 +106,62 @@
 
     far_first = range(n - 1, 0, -1)
 
+    facts_ref[...] = jnp.full(facts_ref.shape, -1, jnp.int32)
+    for i, fact in enumerate(fact_refs):
+        facts_ref[pl.ds(i, 1), pl.ds(0, tile_count)] = fact[...]
+    position = lax.broadcasted_iota(jnp.int32, (1, taps), 1)
+    a_iota = lax.broadcasted_iota(jnp.int32, (rows, rows), 0)
+    b_iota = lax.broadcasted_iota(jnp.int32, (rows, rows), 1)
+    tap_at = b_iota - a_iota + taps // 2
+    inside = jnp.logical_and(tap_at >= 0, tap_at < taps)
+    low = lax.broadcasted_iota(jnp.int32, (2 * rows, LANES), 1) < half
+
+    def toeplitz(d, which):
+        kept = jnp.where(position < len_ref[d], taps_ref[which, pl.ds(d, 1), :], 0.0)
+        rolled = pltpu.roll(jnp.broadcast_to(kept, (rows, taps)), taps // 2, 1, stride=1, stride_axis=0)
+        return jnp.where(inside, jnp.concatenate([rolled] * (rows // taps), axis=1), 0.0)
+
     for h in range(PHASES):
+        for d in range(dates_here):
+            if h == 0:
+                t_re, t_im = toeplitz(d, 0), toeplitz(d, 1)
+                operator_ref[d] = jnp.concatenate(
+                    [jnp.concatenate([t_re, -t_im], axis=1), jnp.concatenate([t_im, t_re], axis=1)], axis=0
+                ).astype(jnp.bfloat16)
+            columns = jnp.concatenate([radar_ref[0, d], radar_ref[1, d]], axis=0).astype(jnp.float32)
+            sides = [columns[:, c * LANES : (c + 1) * LANES] for c in range(2)]
+            sides[1 - h] = pltpu.roll(sides[1 - h], half, 1)
+            product = jnp.dot(
+                operator_ref[d],
+                jnp.where(low, sides[0], sides[1]).astype(jnp.bfloat16),
+                preferred_element_type=jnp.float32,
+            )
+            for p in range(n):
+                for part in range(2):
+                    top = part * rows + p * PATCH_AZ
+                    cell_ref[p, pl.ds(part * PATCH_AZ * dates_here + d, PATCH_AZ, stride=dates_here), :] = product[
+                        top : top + PATCH_AZ
+                    ]
+        for p in range(n):
+            cells_ref[h, p] = cell_ref[p].astype(jnp.bfloat16)
+        if h == 0:
+            pl.semaphore_wait(barrier, n - 1)
         for k in far_first:
             cell_copy(h, partner(k), me).start()
+        own[h].start()
         if h == 0:
             for k in far_first:
                 fact_copy(partner(k), me).start()
+            own[PHASES].start()
+
+    owners = [owner_ref[t] for t in range(tile_count)]
+    for o in range(n):
+        first, last = 0, 0
+        for t in range(tile_count):
+            last = jnp.where(owners[t] == o, t, last)
+            first = jnp.where(owners[tile_count - 1 - t] == o, tile_count - 1 - t, first)
+        table_ref[o * CAP] = first
+        table_ref[o * CAP + 1] = last
 
     per_half = windows // 2
     for h in range(PHASES):
@@ -249,14 +240,16 @@
     gather(me)
 
     def arrive(i, carry):
-        s = partner(n - i)
+        s = partner(i)
         fact_copy(s, s).wait_recv()
         for h in range(PHASES):
             msg_copy(h, s, s).wait_recv()
         gather(s)
         return carry
 
-    lax.fori_loop(1, n, arrive, 0)
+    near = min(4, n)
+    lax.fori_loop(1, near, arrive, 0)
+    lax.fori_loop(near, n, lambda i, carry: arrive(n - 1 + near - i, carry), 0)
     for m in range(MAP_DEV):
         result_ref[m] = (total_ref[m] / jnp.maximum(den_ref[m : m + 1, :1], 1.0)).T
     for k in far_first:
@@ -274,27 +267,16 @@
     message = (PHASES, n, LANES, 2 * dates)
     facts = [x.reshape(1, tile_count) for x in (tile_owner, map_slot, offsets, correlation)]
 
-    cells, known, table = pl.pallas_call(
-        partial(filter_kernel, n),
-        out_shape=[
-            jax.ShapeDtypeStruct(block, jnp.bfloat16),
-            jax.ShapeDtypeStruct((8, LANES), jnp.int32),
-            jax.ShapeDtypeStruct((n * CAP,), jnp.int32),
-        ],
-        in_specs=[SMEM, SMEM] + [VMEM] * 6,
-        out_specs=[VMEM, VMEM, SMEM],
-        scratch_shapes=[pltpu.VMEM(block, jnp.float32), pltpu.SMEM((n,), jnp.int32)],
-        compiler_params=pltpu.CompilerParams(vmem_limit_bytes=BIG),
-        name="filter",
-    )(filter_lengths, tile_owner.reshape(tile_count), radar_stack, filter_taps, *facts)
     dma = pltpu.SemaphoreType.DMA
     return pl.pallas_call(
         partial(flow_kernel, n),
         out_shape=jax.ShapeDtypeStruct((MAP_DEV, 2 * dates, TILE), jnp.float32),
-        in_specs=[SMEM, SMEM, VMEM, VMEM],
+        in_specs=[SMEM, SMEM, SMEM] + [VMEM] * 6,
         out_specs=VMEM,
         scratch_shapes=[
             pltpu.VMEM(block, jnp.bfloat16),
+            pltpu.VMEM(block, jnp.bfloat16),
+            pltpu.VMEM((8, LANES), jnp.int32),
             pltpu.VMEM((n, 8, LANES), jnp.int32),
             pltpu.VMEM(block[1:], jnp.float32),
             pltpu.VMEM((LANES // PATCH_RG, LANES, 2 * dates), jnp.bfloat16),
@@ -303,6 +285,8 @@
             pltpu.VMEM(message, jnp.bfloat16),
             pltpu.VMEM((MAP_DEV, TILE, 2 * dates), jnp.float32),
             pltpu.VMEM((MAP_DEV, TILE), jnp.float32),
+            pltpu.VMEM((dates_here, 2 * rows, 2 * rows), jnp.bfloat16),
+            pltpu.SMEM((n * CAP,), jnp.int32),
             dma((PHASES + 1,)),
             dma((n,)),
             dma((n,)),
@@ -313,7 +297,7 @@
         ],
         compiler_params=pltpu.CompilerParams(collective_id=0, has_side_effects=True, vmem_limit_bytes=BIG),
         name="flow",
-    )(table, resample_kernel, cells, known)
+    )(filter_lengths, tile_owner.reshape(tile_count), resample_kernel, radar_stack, filter_taps, *facts)
 
 
 def solution(mesh):

time: 91.5 us -> 87.8 us (0.960)
  Pallas kernels: 89 us -> 82 us
  local copies, waits for them, and re-layouts: 2.27 us -> 5.52 us
    pallas_call x1 -> x0, Pallas kernels: 3.86 us -> none  [shards(): pl.pallas_call(partial(filter_kernel, n), out_shape=[jax.ShapeDtypeStruct...]
    unnamed x1 -> x17, local copies, waits for them, and re-layouts: 2.27 us -> 5.52 us
    pallas_call x1, Pallas kernels: 85.1 us -> 82 us  [shards(): pl.pallas_call(partial(flow_kernel, n), out_shape=jax.ShapeDtypeStruct((M...]
where the time goes in v3:
time: 87.8 us; the launch traced here: 87.5 us
  Pallas kernels  82 us (93%)
  local copies, waits for them, and re-layouts  5.52 us (6%)
    pallas_call x1, Pallas kernels, shards(): pl.pallas_call(partial(flow_kernel, n), out_shape=jax.ShapeDtypeStruct((M...  82 us
    unnamed x17, local copies, waits for them, and re-layouts  5.52 us

profile of v3, /device:TPU:0, one launch (start us, length us, event | category | flops | bytes accessed | tf_op | source)
XLA Modules:
  0.0 87.5 jit_solution(13634961197870019708)
XLA Ops:
  0.0 0.0 copy-start.1
  0.0 0.0 copy-start.2
  0.0 0.0 copy-start.3
  0.0 0.7 copy-done.1
  0.7 0.0 copy-done.2
  0.7 0.0 copy-done.3
  0.7 0.0 copy-start
  0.7 1.2 %copy-done = bf16[2,8,128,256]{3,2,1,0:T(8,128)(2,1)S(1)} copy-done((bf16[2,8,128,256]{3,2,1,0:T(8,128)(2,1)S(1)}, bf16[2,8,128,256]{3,2,1,0:T(8,128)(2,1)}, u32[]{:S(2)}) %copy-start) | copy-done | bytes 1048600
  1.9 0.0 copy-start.4
  1.9 0.7 copy-done.4
  2.6 0.0 copy-start.5
  2.6 0.7 copy-done.5
  3.2 0.0 copy-start.6
  3.2 0.7 copy-done.6
  3.9 0.0 copy-start.7
  3.9 0.7 copy-done.7
  4.6 82.0 %flow.1 = f32[8,256,128]{2,1,0:T(8,128)S(1)} custom-call(s32[8]{0:T(128)S(1)} %copy-done.3, s32[16]{0:T(128)S(1)} %bitcast.5, f32[4]{0:T(128)S(1)} %copy-done.4, bf16[2,8,128,256]{3,2,1,0:T(8,128)(2,1)S(1)} %copy-done, f32[2,8,128]{2,1,0:T(8,128)S(1)} %copy-done.1, s32[1,16]{1,0:T(1,128)S(1)} %bitcast.6, s32[1,16]{1,0:T(1,128)S(1)} %bitcast.7, ...), custom_call_target="tpu_custom_call" | custom-call | tf_op jit(solution)/shard_map/flow/pallas_call | solution.py:271
  86.6 1.0 %copy.10 = f32[8,256,128]{2,1,0:T(8,128)} copy(f32[8,256,128]{2,1,0:T(8,128)S(1)} %flow.1) | data formatting | bytes 2097152
Async XLA Ops:
  0.0 0.7 copy-start.1
  0.0 0.7 copy-start.2
  0.0 0.7 copy-start.3
  0.7 1.2 %copy-start = (bf16[2,8,128,256]{3,2,1,0:T(8,128)(2,1)S(1)}, bf16[2,8,128,256]{3,2,1,0:T(8,128)(2,1)}, u32[]{:S(2)}) copy-start(bf16[2,8,128,256]{3,2,1,0:T(8,128)(2,1)} %radar_ref.1) | copy-start | bytes 3145732
  1.9 0.7 copy-start.4
  2.6 0.7 copy-start.5
  3.2 0.7 copy-start.6
  3.9 0.7 copy-start.7

commit v4 on v3

--- a/solution.py
+++ b/solution.py
@@ -22,7 +22,7 @@
 small_eps = 1e-05
 MESH = pl.DeviceIdType.MESH
 VMEM = pl.BlockSpec(memory_space=pltpu.VMEM)
-SMEM = pl.BlockSpec(memory_space=pltpu.SMEM)
+HBM = pl.BlockSpec(memory_space=pltpu.MemorySpace.HBM)
 BIG = 32 * 1024 * 1024
 
 
@@ -61,11 +61,14 @@
     return (w * over).astype(jnp.bfloat16)
 
 
-def flow_kernel(n, len_ref, owner_ref, kern_ref, radar_ref, taps_ref, *refs):
-    fact_refs, refs = refs[:4], refs[4:]
+def flow_kernel(n, *refs):
+    inputs, refs = refs[:9], refs[9:]
     result_ref, cells_ref, got_cells, facts_ref, got_facts, cell_ref, z_ref, tiles_ref, out_msg, got_msg = refs[:10]
     total_ref, den_ref, operator_ref, table_ref = refs[10:14]
-    own_sem, fact_send, fact_recv, cell_send, cell_recv, msg_send, msg_recv = refs[14:]
+    local, refs = refs[14:23], refs[23:]
+    len_ref, owner_ref, kern_ref, radar_ref, taps_ref = local[:5]
+    fact_refs = local[5:]
+    own_sem, fact_send, fact_recv, cell_send, cell_recv, msg_send, msg_recv, load_sem = refs
     me = lax.axis_index("date")
     dates_here, rows = radar_ref.shape[1], radar_ref.shape[2]
     taps, tile_count = taps_ref.shape[2], owner_ref.shape[0]
@@ -74,6 +77,9 @@
     windows = LANES // PATCH_RG
 
     barrier = pltpu.get_barrier_semaphore()
+    loads = [pltpu.make_async_copy(x, y, load_sem.at[i]) for i, (x, y) in enumerate(zip(inputs, local))]
+    for load in loads:
+        load.start()
     for k in range(1, n):
         pl.semaphore_signal(barrier, inc=1, device_id={"date": lax.rem(me + k, n)}, device_id_type=MESH)
     own = [pltpu.make_async_copy(cells_ref.at[h, me], got_cells.at[h, me], own_sem.at[h]) for h in range(PHASES)]
@@ -104,8 +110,13 @@
             bit *= 2
         return peer
 
-    far_first = range(n - 1, 0, -1)
-
+    def turn(i):
+        return n - 1 - i // 2 - i % 2 * (n // 2)
+
+    peers = [turn(i) for i in range(n - 1)]
+
+    for load in loads:
+        load.wait()
     facts_ref[...] = jnp.full(facts_ref.shape, -1, jnp.int32)
     for i, fact in enumerate(fact_refs):
         facts_ref[pl.ds(i, 1), pl.ds(0, tile_count)] = fact[...]
@@ -146,11 +157,11 @@
             cells_ref[h, p] = cell_ref[p].astype(jnp.bfloat16)
         if h == 0:
             pl.semaphore_wait(barrier, n - 1)
-        for k in far_first:
+        for k in peers:
             cell_copy(h, partner(k), me).start()
         own[h].start()
         if h == 0:
-            for k in far_first:
+            for k in peers:
                 fact_copy(partner(k), me).start()
             own[PHASES].start()
 
@@ -166,7 +177,7 @@
     per_half = windows // 2
     for h in range(PHASES):
         own[h].wait()
-        for k in far_first:
+        for k in peers:
             cell_copy(h, partner(k), partner(k)).wait_recv()
         for s in range(n):
             cell_ref[s] = got_cells[h, s].astype(jnp.float32)
@@ -204,7 +215,7 @@
         lax.fori_loop(1, n, pack, 0)
         for i in range(CAP):
             got_msg[h, me, pl.ds(i * half, half), :] = message(me, i)
-        for k in far_first:
+        for k in peers:
             msg_copy(h, partner(k), me).start()
 
     total_ref[...] = jnp.zeros(total_ref.shape, jnp.float32)
@@ -240,19 +251,17 @@
     gather(me)
 
     def arrive(i, carry):
-        s = partner(i)
+        s = partner(turn(i))
         fact_copy(s, s).wait_recv()
         for h in range(PHASES):
             msg_copy(h, s, s).wait_recv()
         gather(s)
         return carry
 
-    near = min(4, n)
-    lax.fori_loop(1, near, arrive, 0)
-    lax.fori_loop(near, n, lambda i, carry: arrive(n - 1 + near - i, carry), 0)
+    lax.fori_loop(0, n - 1, arrive, 0)
     for m in range(MAP_DEV):
         result_ref[m] = (total_ref[m] / jnp.maximum(den_ref[m : m + 1, :1], 1.0)).T
-    for k in far_first:
+    for k in peers:
         fact_copy(partner(k), me).wait_send()
         for h in range(PHASES):
             cell_copy(h, partner(k), me).wait_send()
@@ -271,7 +280,7 @@
     return pl.pallas_call(
         partial(flow_kernel, n),
         out_shape=jax.ShapeDtypeStruct((MAP_DEV, 2 * dates, TILE), jnp.float32),
-        in_specs=[SMEM, SMEM, SMEM] + [VMEM] * 6,
+        in_specs=[HBM] * 9,
         out_specs=VMEM,
         scratch_shapes=[
             pltpu.VMEM(block, jnp.bfloat16),
@@ -287,6 +296,15 @@
             pltpu.VMEM((MAP_DEV, TILE), jnp.float32),
             pltpu.VMEM((dates_here, 2 * rows, 2 * rows), jnp.bfloat16),
             pltpu.SMEM((n * CAP,), jnp.int32),
+            pltpu.SMEM(filter_lengths.shape, jnp.int32),
+            pltpu.SMEM((tile_count,), jnp.int32),
+            pltpu.SMEM(resample_kernel.shape, jnp.float32),
+            pltpu.VMEM(radar_stack.shape, radar_stack.dtype),
+            pltpu.VMEM(filter_taps.shape, jnp.float32),
+            pltpu.VMEM((1, tile_count), jnp.int32),
+            pltpu.VMEM((1, tile_count), jnp.int32),
+            pltpu.VMEM((1, tile_count), jnp.int32),
+            pltpu.VMEM((1, tile_count), jnp.int32),
             dma((PHASES + 1,)),
             dma((n,)),
             dma((n,)),
@@ -294,10 +312,11 @@
             dma((PHASES, n)),
             dma((PHASES, n)),
             dma((PHASES, n)),
+            dma((9,)),
         ],
         compiler_params=pltpu.CompilerParams(collective_id=0, has_side_effects=True, vmem_limit_bytes=BIG),
         name="flow",
-    )(filter_lengths, tile_owner.reshape(tile_count), resample_kernel, radar_stack, filter_taps, *facts)
+    )(*[pltpu.with_memory_space_constraint(x, pltpu.MemorySpace.HBM) for x in (filter_lengths, tile_owner.reshape(tile_count), resample_kernel, radar_stack, filter_taps, *facts)])
 
 
 def solution(mesh):

time: 87.8 us -> 80.2 us (0.913)
  local copies, waits for them, and re-layouts: 5.52 us -> 0.97 us
  Pallas kernels: 82 us -> 79.1 us
    unnamed x17 -> x1, local copies, waits for them, and re-layouts: 5.52 us -> 0.97 us
    pallas_call x1, Pallas kernels: 82 us -> 79.1 us  [shards(): pl.pallas_call(partial(flow_kernel, n), out_shape=jax.ShapeDtypeStruct((M...]
where the time goes in v4:
time: 80.2 us; the launch traced here: 80.1 us
  Pallas kernels  79.1 us (99%)
  local copies, waits for them, and re-layouts  0.97 us (1%)
    pallas_call x1, Pallas kernels, shards(): pl.pallas_call(partial(flow_kernel, n), out_shape=jax.ShapeDtypeStruct((M...  79.1 us

profile of v4, /device:TPU:0, one launch (start us, length us, event | category | flops | bytes accessed | tf_op | source)
XLA Modules:
  0.0 80.1 jit_solution(6635232067667068726)
XLA Ops:
  0.0 79.1 %flow.1 = f32[8,256,128]{2,1,0:T(8,128)S(1)} custom-call(s32[8]{0:T(128)} %refs_0_.1, s32[16]{0:T(128)} %bitcast.5, f32[4]{0:T(128)} %refs_2_.1, bf16[2,8,128,256]{3,2,1,0:T(8,128)(2,1)} %refs_3_.1, f32[2,8,128]{2,1,0:T(8,128)} %refs_4_.1, s32[1,16]{1,0:T(1,128)} %bitcast.6, s32[1,16]{1,0:T(1,128)} %bitcast.7, s32[1,16]{1,0:T(1,128)} %bitcast.8, s32[1,16]{1,0:T(1,128)} %bitcast.9), custom_call_target="tpu_custom_call" | custom-call | tf_op jit(solution)/shard_map/flow/pallas_call | solution.py:280
  79.1 1.0 %copy.10 = f32[8,256,128]{2,1,0:T(8,128)} copy(f32[8,256,128]{2,1,0:T(8,128)S(1)} %flow.1) | data formatting | bytes 2097152

commit v5 on v4

--- a/solution.py
+++ b/solution.py
@@ -115,6 +115,7 @@
 
     peers = [turn(i) for i in range(n - 1)]
 
+    radar_load = loads.pop(3)
     for load in loads:
         load.wait()
     facts_ref[...] = jnp.full(facts_ref.shape, -1, jnp.int32)
@@ -139,6 +140,8 @@
                 operator_ref[d] = jnp.concatenate(
                     [jnp.concatenate([t_re, -t_im], axis=1), jnp.concatenate([t_im, t_re], axis=1)], axis=0
                 ).astype(jnp.bfloat16)
+            if h == 0 and d == 0:
+                radar_load.wait()
             columns = jnp.concatenate([radar_ref[0, d], radar_ref[1, d]], axis=0).astype(jnp.float32)
             sides = [columns[:, c * LANES : (c + 1) * LANES] for c in range(2)]
             sides[1 - h] = pltpu.roll(sides[1 - h], half, 1)

time: 80.2 us -> 80.2 us (level)
  no operation moved by 1% of the time
where the time goes in v5:
time: 80.2 us; the launch traced here: 80.1 us
  Pallas kernels  79.1 us (99%)
  local copies, waits for them, and re-layouts  0.97 us (1%)
    pallas_call x1, Pallas kernels, shards(): pl.pallas_call(partial(flow_kernel, n), out_shape=jax.ShapeDtypeStruct((M...  79.1 us

profile of v5, /device:TPU:0, one launch (start us, length us, event | category | flops | bytes accessed | tf_op | source)
XLA Modules:
  0.0 80.1 jit_solution(12326251435672989315)
XLA Ops:
  0.0 79.1 %flow.1 = f32[8,256,128]{2,1,0:T(8,128)S(1)} custom-call(s32[8]{0:T(128)} %refs_0_.1, s32[16]{0:T(128)} %bitcast.5, f32[4]{0:T(128)} %refs_2_.1, bf16[2,8,128,256]{3,2,1,0:T(8,128)(2,1)} %refs_3_.1, f32[2,8,128]{2,1,0:T(8,128)} %refs_4_.1, s32[1,16]{1,0:T(1,128)} %bitcast.6, s32[1,16]{1,0:T(1,128)} %bitcast.7, s32[1,16]{1,0:T(1,128)} %bitcast.8, s32[1,16]{1,0:T(1,128)} %bitcast.9), custom_call_target="tpu_custom_call" | custom-call | tf_op jit(solution)/shard_map/flow/pallas_call | solution.py:283
  79.1 1.0 %copy.10 = f32[8,256,128]{2,1,0:T(8,128)} copy(f32[8,256,128]{2,1,0:T(8,128)S(1)} %flow.1) | data formatting | bytes 2097152
